TPU v7x, 32 devices: a whole 2x2x4 slice. The times are simulated.
32 devices in a mesh: blk: 16 (over z, y, core), map: 2 (over x).
Axes of the slice: x: 2, y: 2, z: 4, core: 2. Of those that a mesh axis runs over, the one named last changes fastest.
Arguments:
- phase_history: bfloat16 [16, 2, 128, 1024], P('blk', 'map'), may hold values from -6 to 6
- tile_curvature: float32 [16], P('blk'), may hold values from 20 to 80
- interp_weights: bfloat16 [16, 512, 512], P('blk'), may hold values from -0.25 to 0.25
- strip_tiles: int32 [16, 2, 256, 1], P('blk', 'map'), may hold values from 0 to 15; in each aligned block of 256 rows (0 to 255, 256 to 511, ..., all dimensions but the last counted through in order) at most 32 rows name the same one
- row_offsets: int32 [16, 2, 256], P('blk', 'map'), may hold values from 0 to 255
- tile_owner: int32 [16], replicated, may hold values from 0 to 15, each once
Outputs:
- map_power: float32 [16, 2, 256, 512], P('blk', 'map')
Inputs may be any that keep to these rules, and one draw needn't show every extreme that they name: `strip_tiles`: among the rows of one device no map tile is named more than 32 times, and in every draw some device names some tile exactly 32 times. `tile_owner`: every blk index holds exactly one map tile.
All inputs are finite; a program needn't handle non-finite values.
Results may differ from a plain program's by a relative error of at most 0.0055.
Values may be sent and summed in bfloat16 or wider, within the bound.
A program may use at most 64 MiB of HBM per device.

v0:
```python
import math

import jax
import jax.numpy as jnp
from jax import lax
from jax.sharding import PartitionSpec as P

STOPS = 8
MAPH = 256


def from_behind(block, axis, distance):
    devices = range(lax.axis_size(axis))
    route = [((i - distance) % len(devices), i) for i in devices]
    return lax.ppermute(block, axis, route)


def range_matrix(freq_count, column_count):
    freq_index = jnp.arange(freq_count, dtype=jnp.int32)[:, None]
    column_index = jnp.arange(column_count, dtype=jnp.int32)[None, :]
    angle = (freq_index * column_index % freq_count).astype(jnp.float32) * (
        2.0 * math.pi / freq_count
    )
    factor = 1.0 / math.sqrt(freq_count)
    real_part = jnp.cos(angle) * factor
    imag_part = -jnp.sin(angle) * factor
    upper = jnp.concatenate([real_part, imag_part], axis=1)
    lower = jnp.concatenate([-imag_part, real_part], axis=1)
    return jnp.concatenate([upper, lower], axis=0).astype(jnp.bfloat16)


def cross_rows(stop_index, map_index, row_index, map_count, pulse_count, span):
    pulse_index = jnp.arange(pulse_count, dtype=jnp.int32)[None, :]
    along = (stop_index * map_count + map_index) * pulse_count + pulse_index
    angle = (row_index[:, None] * along % span).astype(jnp.float32) * (2.0 * math.pi / span)
    factor = 1.0 / math.sqrt(span)
    return jnp.concatenate([jnp.cos(angle) * factor, -jnp.sin(angle) * factor], axis=1).astype(
        jnp.bfloat16
    )


def apply_phase(
    source_block, curvature, stop_index, map_index, map_count, pulse_count, freq_count, span
):
    pulse_index = jnp.arange(pulse_count, dtype=jnp.int32)
    along = ((stop_index * map_count + map_index) * pulse_count + pulse_index).astype(
        jnp.float32
    ) / span - 0.5
    relative = jnp.arange(freq_count, dtype=jnp.int32).astype(jnp.float32) / freq_count - 0.5
    phase_angle = curvature * (along * along)[:, None] * (1.0 + relative[None, :])
    cosine = jnp.cos(phase_angle)
    sine = jnp.sin(phase_angle)
    values = source_block.astype(jnp.float32)
    real_part = values[:, :freq_count]
    imag_part = values[:, freq_count:]
    return jnp.concatenate(
        [real_part * cosine - imag_part * sine, real_part * sine + imag_part * cosine], axis=1
    ).astype(jnp.bfloat16)


def stack_spectrum(spectrum_now):
    half_width = spectrum_now.shape[1] // 2
    real_part = spectrum_now[:, :half_width]
    imag_part = spectrum_now[:, half_width:]
    upper = jnp.concatenate([real_part, imag_part], axis=1)
    lower = jnp.concatenate([-imag_part, real_part], axis=1)
    return jnp.concatenate([upper, lower], axis=0)


def body(phase_history, tile_curvature, interp_weights, strip_tiles, row_offsets, tile_owner):
    blk_count = lax.axis_size("blk")
    map_count = lax.axis_size("map")
    here_map = lax.axis_index("map")
    own_block = phase_history[0, 0]
    pulse_count = own_block.shape[0]
    freq_count = own_block.shape[1] // 2
    columns = interp_weights.shape[2]
    rows_here = strip_tiles.shape[2]
    tile_rows = rows_here * map_count
    span = STOPS * map_count * pulse_count
    curvature = tile_curvature[0]
    ranges = range_matrix(freq_count, columns)
    lead_count = STOPS // 2 - 1
    every_row = jnp.arange(tile_rows, dtype=jnp.int32)

    def spectrum_of(stop_index, arrived):
        phased = apply_phase(
            arrived, curvature, stop_index, here_map, map_count, pulse_count, freq_count, span
        )
        return jnp.dot(phased, ranges, preferred_element_type=jnp.float32).astype(jnp.bfloat16)

    def accumulate(running, stop_index, arrived):
        spectrum_now = spectrum_of(stop_index, arrived)
        left_side = cross_rows(stop_index, here_map, every_row, map_count, pulse_count, span)
        right_side = stack_spectrum(spectrum_now)
        return running + jnp.dot(left_side, right_side, preferred_element_type=jnp.float32)

    running = jnp.zeros((tile_rows, 2 * columns), jnp.float32)
    running = accumulate(running, lead_count, own_block)
    current = own_block
    for turn_index in range(lead_count):
        current = from_behind(current, "blk", 1)
        running = accumulate(running, lead_count - 1 - turn_index, current)
    current = own_block
    for turn_index in range(STOPS - lead_count - 1):
        current = from_behind(current, "blk", -1)
        running = accumulate(running, lead_count + 1 + turn_index, current)
    image_rows = lax.psum_scatter(running, "map", scatter_dimension=0, tiled=True).astype(
        jnp.bfloat16
    )
    capacity = max(2, 2 * rows_here // blk_count)
    holder_index = jnp.arange(blk_count, dtype=jnp.int32)
    row_tiles = strip_tiles[0, 0, :, 0]
    own_offsets = row_offsets[0, 0]
    tile_match = row_tiles[:, None] == holder_index[None, :]
    destination = jnp.sum(jnp.where(tile_match, tile_owner[None, :], 0), axis=1)
    dest_hot = (destination[:, None] == holder_index[None, :]).astype(jnp.int32)
    rank_within = jnp.sum(jnp.cumsum(dest_hot, axis=0) * dest_hot, axis=1) - 1
    slot_index = destination * capacity + rank_within
    slot_hot = jnp.arange(blk_count * capacity, dtype=jnp.int32)[:, None] == slot_index[None, :]
    packed = jnp.dot(
        slot_hot.astype(jnp.bfloat16), image_rows, preferred_element_type=jnp.float32
    ).astype(jnp.bfloat16)
    slot_offsets = jnp.sum(jnp.where(slot_hot, own_offsets[None, :] + 1, 0), axis=1) - 1
    packed = packed.reshape(blk_count, capacity, 2 * columns)
    slot_offsets = slot_offsets.reshape(blk_count, capacity)
    weights = interp_weights[0]
    arrived_rows = lax.all_to_all(packed, "blk", split_axis=0, concat_axis=0, tiled=True)
    arrived_offsets = lax.all_to_all(slot_offsets, "blk", split_axis=0, concat_axis=0, tiled=True)
    split_rows = arrived_rows.reshape(arrived_rows.shape[0], arrived_rows.shape[1], 2, columns)
    mapped = jnp.einsum("sikc,cd->sikd", split_rows, weights, preferred_element_type=jnp.float32)
    power_rows = jnp.sum(mapped * mapped, axis=2)
    flat_power = power_rows.reshape(-1, columns)
    flat_offsets = arrived_offsets.reshape(-1)
    place_hot = (jnp.arange(MAPH, dtype=jnp.int32)[:, None] == flat_offsets[None, :]).astype(
        jnp.float32
    )
    tile_map = jnp.dot(
        place_hot, flat_power, precision=lax.Precision.HIGHEST, preferred_element_type=jnp.float32
    )
    return tile_map.reshape(1, 1, MAPH, columns)


def solution(mesh):
    in_specs = (
        P("blk", "map", None, None),
        P("blk"),
        P("blk", None, None),
        P("blk", "map", None, None),
        P("blk", "map", None),
        P(),
    )
    out_specs = P("blk", "map", None, None)
    return jax.shard_map(body, mesh=mesh, in_specs=in_specs, out_specs=out_specs, check_vma=False)
```

profile of v0, /device:TPU:0, one launch (start us, length us, event | category | flops | bytes accessed | tf_op | source)
XLA Modules:
  0.0 142.1 jit_solution(18436589131131787490)
XLA Ops:
  7.0 5.0 %collective-permute-start.3 = (bf16[128,1024]{1,0:T(8,128)(2,1)}, bf16[128,1024]{1,0:T(8,128)(2,1)S(1)}, u32[]{:S(2)}, u32[]{:S(2)}) collective-permute-start(bf16[128,1024]{1,0:T(8,128)(2,1)} %bitcast.45), channel_id=1, source_target_pairs={{2,0},{4,2},{6,4},{8,6},{10,8},{12,10},{14,12},{16,14},{18,16},{20... | collective-permute-start | bytes 786440 | tf_op jit(solution)/shard_map/ppermute | solution.py:15
  12.1 4.0 %fusion.8 = bf16[512,512]{1,0:T(8,128)(2,1)S(1)} fusion(), kind=kLoop, calls=%fused_computation.27 | loop fusion | flops 4456448 | bytes 524288 | tf_op jit(solution)/shard_map/convert.33
  16.1 4.4 %negate_convert_fusion = (bf16[512,512]{1,0:T(8,128)(2,1)S(1)}, bf16[512,512]{1,0:T(8,128)(2,1)S(1)}) fusion(), kind=kLoop, calls=%fused_computation.21 | loop fusion | flops 5242880 | bytes 1048576 | tf_op jit(solution)/shard_map/convert.30
  21.3 1.1 multiply_convert_fusion.2
  22.4 1.1 multiply_convert_fusion.4
  23.6 1.1 multiply_convert_fusion.8
  24.7 1.1 multiply_convert_fusion.10
  25.8 1.1 multiply_convert_fusion.12
  28.1 1.1 multiply_convert_fusion.6
  30.6 4.5 %collective-permute-start.4 = (bf16[128,1024]{1,0:T(8,128)(2,1)S(1)}, bf16[128,1024]{1,0:T(8,128)(2,1)S(1)}, u32[]{:S(2)}, u32[]{:S(2)}) collective-permute-start(bf16[128,1024]{1,0:T(8,128)(2,1)S(1)} %collective-permute-done.3), channel_id=1, source_target_pairs={{2,0},{4,2},{6,4},{8,6},{10,8},{12,10},{14,12},{16,14},{18,16},{20... | collective-permute-start | bytes 786440 | tf_op jit(solution)/shard_map/ppermute | solution.py:15
  35.1 3.8 %collective-permute-done.1 = bf16[128,1024]{1,0:T(8,128)(2,1)S(1)} collective-permute-done((bf16[128,1024]{1,0:T(8,128)(2,1)S(1)}, bf16[128,1024]{1,0:T(8,128)(2,1)S(1)}, u32[]{:S(2)}, u32[]{:S(2)}) %collective-permute-start.1) | collective-permute-done | bytes 262176 | tf_op jit(solution)/shard_map/ppermute | solution.py:15
  39.0 2.3 %fusion.119 = (bf16[128,512]{1,0:T(8,128)(2,1)S(1)}, bf16[128,512]{1,0:T(8,128)(2,1)S(1)}, bf16[128,512]{1,0:T(8,128)(2,1)S(1)}, bf16[128,512]{1,0:T(8,128)(2,1)S(1)}) fusion(f32[128,1024]{1,0:T(8,128)S(1)} %bitcast_convert_fusion, f32[512]{0:T(512)S(1)} %multiply_add_fusion, f32[128]{0:T(128)S(1)} %get-tuple-element.68, ...), kind=kLoop, calls=%fused_computation.181 | loop fusion | flops 1179648 | bytes 1575936 | tf_op jit(solution)/shard_map/convert.34
  42.4 4.5 %collective-permute-start.5 = (bf16[128,1024]{1,0:T(8,128)(2,1)S(1)}, bf16[128,1024]{1,0:T(8,128)(2,1)S(1)}, u32[]{:S(2)}, u32[]{:S(2)}) collective-permute-start(bf16[128,1024]{1,0:T(8,128)(2,1)S(1)} %collective-permute-done.4), channel_id=1, source_target_pairs={{2,0},{4,2},{6,4},{8,6},{10,8},{12,10},{14,12},{16,14},{18,16},{20... | collective-permute-start | bytes 786440 | tf_op jit(solution)/shard_map/ppermute | solution.py:15
  47.8 3.0 %collective-permute-done.2 = bf16[128,1024]{1,0:T(8,128)(2,1)S(1)} collective-permute-done((bf16[128,1024]{1,0:T(8,128)(2,1)S(1)}, bf16[128,1024]{1,0:T(8,128)(2,1)S(1)}, u32[]{:S(2)}, u32[]{:S(2)}) %collective-permute-start.2) | collective-permute-done | bytes 262176 | tf_op jit(solution)/shard_map/ppermute | solution.py:15
  50.9 3.3 %fusion.115 = (bf16[128,512]{1,0:T(8,128)(2,1)S(1)}, bf16[128,512]{1,0:T(8,128)(2,1)S(1)}, bf16[128,512]{1,0:T(8,128)(2,1)S(1)}, bf16[128,512]{1,0:T(8,128)(2,1)...) fusion(f32[128,1024]{1,0:T(8,128)S(1)} %convert_element_type.203, f32[128]{0:T(128)S(1)} %multiply_multiply_fusion.6, ...), kind=kLoop, calls=%fused_computation.177 | loop fusion | flops 1769472 | bytes 2362880 | tf_op jit(solution)/shard_map/convert.24
  57.3 2.9 %collective-permute-done.6 = bf16[128,1024]{1,0:T(8,128)(2,1)S(1)} collective-permute-done((bf16[128,1024]{1,0:T(8,128)(2,1)S(1)}, bf16[128,1024]{1,0:T(8,128)(2,1)S(1)}, u32[]{:S(2)}, u32[]{:S(2)}) %collective-permute-start.6) | collective-permute-done | bytes 262176 | tf_op jit(solution)/shard_map/ppermute | solution.py:15
  60.3 3.3 %fusion.91 = (bf16[128,512]{1,0:T(8,128)(2,1)S(1)}, bf16[128,512]{1,0:T(8,128)(2,1)S(1)}, bf16[128,512]{1,0:T(8,128)(2,1)S(1)}, bf16[128,512]{1,0:T(8,128)(2,1)S...) fusion(f32[128,1024]{1,0:T(8,128)S(1)} %convert_element_type.227, f32[128]{0:T(128)S(1)} %get-tuple-element.63, ...), kind=kLoop, calls=%fused_computation.153 | loop fusion | flops 1769472 | bytes 2362880 | tf_op jit(solution)/shard_map/convert
  65.9 2.1 %add_add_fusion = f32[512,1024]{1,0:T(8,128)} fusion(f32[512,1024]{1,0:T(8,128)S(1)} %fusion.45, f32[512,1024]{1,0:T(8,128)S(1)} %fusion.39, f32[512,1024]{1,0:T(8,128)S(1)} %fusion.33, f32[512,1024]{1,0:T(8,128)S(1)} %fusion.27, f32[512,1024]{1,0:T(8,128)S(1)} %fusion.21, f32[512,1024]{1,0:T(8,128)S(1)} %fusion.9, f32[512,1024]{1,0:T(8,128)S(1)} %fusion.15, ...), kind=kOutput, calls=%fused_computation.2 | convolution fusion | flops 274202624 | bytes 17563648 | tf_op jit(solution)/shard_map/dot_general | solution.py:96
  70.6 6.0 %all-to-all-start = ((s32[16,1,32]{2,1,0:T(1,128)}), s32[16,1,32]{2,1,0:T(1,128)S(1)}, u32[]{:S(2)}, u32[]{:S(2)}) async-start(s32[16,1,32]{2,1,0:T(1,128)} %sub.68), calls=%async_computation | async-start | bytes 16384 | tf_op jit(solution)/shard_map/all_to_all | solution.py:129
  76.6 25.3 %reduce-scatter.2.cloned.1.call-done = f32[256,1024]{1,0:T(8,128)} async-done(((f32[512,1024]{1,0:T(8,128)}), f32[256,1024]{1,0:T(8,128)}) %reduce-scatter.2.cloned.1.call-update) | async-done | bytes 1048592 | tf_op jit(solution)/shard_map/reduce_scatter | solution.py:108
  101.8 2.6 %convolution_convert_fusion = bf16[512,1024]{1,0:T(8,128)(2,1)} fusion(f32[256,1024]{1,0:T(8,128)} %reduce-scatter.2.cloned.1.call-done, s32[256]{0:T(256)S(1)} %add_add_fusion.1), kind=kOutput, calls=%fused_computation.6 | convolution fusion | flops 269352960 | bytes 2098176 | tf_op jit(solution)/shard_map/dot_general | solution.py:121
  104.5 5.6 %all-to-all-start.1 = ((bf16[16,32,1024]{2,1,0:T(8,128)(2,1)}), bf16[16,32,1024]{2,1,0:T(8,128)(2,1)S(1)}, u32[]{:S(2)}, u32[]{:S(2)}) async-start(bf16[16,32,1024]{2,1,0:T(8,128)(2,1)} %bitcast.6), calls=%async_computation.2 | async-start | bytes 2097152 | tf_op jit(solution)/shard_map/all_to_all | solution.py:128
  111.4 21.6 %all-to-all-done.1 = bf16[16,32,1024]{2,1,0:T(8,128)(2,1)S(1)} async-done(((bf16[16,32,1024]{2,1,0:T(8,128)(2,1)}), bf16[16,32,1024]{2,1,0:T(8,128)(2,1)S(1)}, u32[]{:S(2)}, u32[]{:S(2)}) %all-to-all-start.1) | async-done | bytes 1048608 | tf_op jit(solution)/shard_map/all_to_all | solution.py:128
  133.7 1.5 %convolution_bitcast_fusion = f32[1,1,256,512]{3,2,1,0:T(8,128)} fusion(f32[512,512]{1,0:T(8,128)S(1)} %bitcast.42, s32[512]{0:T(512)S(1)} %eq.92), kind=kOutput, calls=%fused_computation.7 | convolution fusion | flops 805437440 | bytes 1574912 | tf_op jit(solution)/shard_map/dot_general | solution.py:138
  (84 shorter events, 14.9 us)
Async XLA Ops:
  6.5 126.5 %copy-start = (bf16[1,512,512]{2,1,0:T(8,128)(2,1)S(1)}, bf16[1,512,512]{2,1,0:T(8,128)(2,1)}, u32[]{:S(2)}) copy-start(bf16[1,512,512]{2,1,0:T(8,128)(2,1)} %param.8) | copy-start | bytes 1572868
  6.5 24.0 %copy-start.1 = (bf16[1,1,128,1024]{3,2,1,0:T(8,128)(2,1)S(1)}, bf16[1,1,128,1024]{3,2,1,0:T(8,128)(2,1)}, u32[]{:S(2)}) copy-start(bf16[1,1,128,1024]{3,2,1,0:T(8,128)(2,1)} %param.6) | copy-start | bytes 786436
  6.5 95.3 %reduce-scatter.2.cloned.1.call-start = ((), (), s32[]{:S(2)}) async-start(), calls=%async_computation.3 | async-start | bytes 3145728 | tf_op jit(solution)/shard_map/reduce_scatter | solution.py:108
  6.5 23.9 %collective-permute-start = (bf16[128,1024]{1,0:T(8,128)(2,1)}, bf16[128,1024]{1,0:T(8,128)(2,1)S(1)}, u32[]{:S(2)}, u32[]{:S(2)}) collective-permute-start(bf16[128,1024]{1,0:T(8,128)(2,1)} %bitcast.44), channel_id=1, source_target_pairs={{30,0},{0,2},{2,4},{4,6},{6,8},{8,10},{10,12},{12,14},{14,16},{16,... | collective-permute-start | bytes 786440 | tf_op jit(solution)/shard_map/ppermute | solution.py:15
  7.0 23.5 %collective-permute-start.3 = (bf16[128,1024]{1,0:T(8,128)(2,1)}, bf16[128,1024]{1,0:T(8,128)(2,1)S(1)}, u32[]{:S(2)}, u32[]{:S(2)}) collective-permute-start(bf16[128,1024]{1,0:T(8,128)(2,1)} %bitcast.45), channel_id=1, source_target_pairs={{2,0},{4,2},{6,4},{8,6},{10,8},{12,10},{14,12},{16,14},{18,16},{20... | collective-permute-start | bytes 786440 | tf_op jit(solution)/shard_map/ppermute | solution.py:15
  30.4 8.5 %collective-permute-start.1 = (bf16[128,1024]{1,0:T(8,128)(2,1)S(1)}, bf16[128,1024]{1,0:T(8,128)(2,1)S(1)}, u32[]{:S(2)}, u32[]{:S(2)}) collective-permute-start(bf16[128,1024]{1,0:T(8,128)(2,1)S(1)} %collective-permute-done), channel_id=1, source_target_pairs={{30,0},{0,2},{2,4},{4,6},{6,8},{8,10},{10,12},{12,14},{14,16},{16,... | collective-permute-start | bytes 786440 | tf_op jit(solution)/shard_map/ppermute | solution.py:15
  30.6 11.8 %collective-permute-start.4 = (bf16[128,1024]{1,0:T(8,128)(2,1)S(1)}, bf16[128,1024]{1,0:T(8,128)(2,1)S(1)}, u32[]{:S(2)}, u32[]{:S(2)}) collective-permute-start(bf16[128,1024]{1,0:T(8,128)(2,1)S(1)} %collective-permute-done.3), channel_id=1, source_target_pairs={{2,0},{4,2},{6,4},{8,6},{10,8},{12,10},{14,12},{16,14},{18,16},{20... | collective-permute-start | bytes 786440 | tf_op jit(solution)/shard_map/ppermute | solution.py:15
  42.3 8.5 %collective-permute-start.2 = (bf16[128,1024]{1,0:T(8,128)(2,1)S(1)}, bf16[128,1024]{1,0:T(8,128)(2,1)S(1)}, u32[]{:S(2)}, u32[]{:S(2)}) collective-permute-start(bf16[128,1024]{1,0:T(8,128)(2,1)S(1)} %collective-permute-done.1), channel_id=1, source_target_pairs={{30,0},{0,2},{2,4},{4,6},{6,8},{8,10},{10,12},{12,14},{14,16},{16,... | collective-permute-start | bytes 786440 | tf_op jit(solution)/shard_map/ppermute | solution.py:15
  42.4 13.7 %collective-permute-start.5 = (bf16[128,1024]{1,0:T(8,128)(2,1)S(1)}, bf16[128,1024]{1,0:T(8,128)(2,1)S(1)}, u32[]{:S(2)}, u32[]{:S(2)}) collective-permute-start(bf16[128,1024]{1,0:T(8,128)(2,1)S(1)} %collective-permute-done.4), channel_id=1, source_target_pairs={{2,0},{4,2},{6,4},{8,6},{10,8},{12,10},{14,12},{16,14},{18,16},{20... | collective-permute-start | bytes 786440 | tf_op jit(solution)/shard_map/ppermute | solution.py:15
  56.1 4.1 %collective-permute-start.6 = (bf16[128,1024]{1,0:T(8,128)(2,1)S(1)}, bf16[128,1024]{1,0:T(8,128)(2,1)S(1)}, u32[]{:S(2)}, u32[]{:S(2)}) collective-permute-start(bf16[128,1024]{1,0:T(8,128)(2,1)S(1)} %collective-permute-done.5), channel_id=1, source_target_pairs={{2,0},{4,2},{6,4},{8,6},{10,8},{12,10},{14,12},{16,14},{18,16},{20... | collective-permute-start | bytes 786440 | tf_op jit(solution)/shard_map/ppermute | solution.py:15
  68.0 0.7 copy-start.2
  68.0 0.7 copy-start.4
  68.0 1.7 %copy-start.3 = (s32[1,1,256]{2,1,0:T(1,128)S(1)}, s32[1,1,256]{2,1,0:T(1,128)}, u32[]{:S(2)}) copy-start(s32[1,1,256]{2,1,0:T(1,128)} %param.10) | copy-start | bytes 3076
  70.6 33.9 %all-to-all-start = ((s32[16,1,32]{2,1,0:T(1,128)}), s32[16,1,32]{2,1,0:T(1,128)S(1)}, u32[]{:S(2)}, u32[]{:S(2)}) async-start(s32[16,1,32]{2,1,0:T(1,128)} %sub.68), calls=%async_computation | async-start | bytes 16384 | tf_op jit(solution)/shard_map/all_to_all | solution.py:129
  104.5 28.5 %all-to-all-start.1 = ((bf16[16,32,1024]{2,1,0:T(8,128)(2,1)}), bf16[16,32,1024]{2,1,0:T(8,128)(2,1)S(1)}, u32[]{:S(2)}, u32[]{:S(2)}) async-start(bf16[16,32,1024]{2,1,0:T(8,128)(2,1)} %bitcast.6), calls=%async_computation.2 | async-start | bytes 2097152 | tf_op jit(solution)/shard_map/all_to_all | solution.py:128
Sparse Core Ops, SparseCore 0:
  68.2 33.6 reduce-scatter.1
where the time goes:
time: 144 us; the launch traced here: 142 us
  waiting for transfers between devices  56.7 us (39%)
  other arithmetic  28.5 us (20%)
  starting transfers between devices  26.4 us (18%)
  between operations  14.6 us (10%)
  matrix products  13.7 us (10%)
  local copies, waits for them, and re-layouts  2.13 us (1%)
    another operation x15, other arithmetic  27 us
    reduce_scatter x1, waiting for transfers between devices, body(): lax.psum_scatter(running, 'map', scatter_dimension=0, tiled=True)  25.3 us
    all_to_all x1, waiting for transfers between devices, body(): lax.all_to_all(packed, 'blk', split_axis=0, concat_axis=0, tiled=True)  21.6 us
    ppermute x7, starting transfers between devices, from_behind(): return lax.ppermute(block, axis, route)  14.8 us
    ppermute x7, waiting for transfers between devices, from_behind(): return lax.ppermute(block, axis, route)  9.8 us
    all_to_all x1, starting transfers between devices, body(): lax.all_to_all(slot_offsets, 'blk', split_axis=0, concat_axis=0, tiled=True)  5.99 us
    all_to_all x1, starting transfers between devices, body(): lax.all_to_all(packed, 'blk', split_axis=0, concat_axis=0, tiled=True)  5.63 us
    dot_general x8, matrix products, accumulate(): jnp.dot(left_side, right_side, preferred_element_type=jnp.float32)  5.25 us
  transfers between devices with their start and end apart: 10, of which 5 were waited for; matrix products, arithmetic and copies ran while one was open for 24% of the time, Pallas kernels for 0%

commit v1 on v0

v1 whole, which is shorter than its diff:
```python
import functools
import math

import jax
import jax.numpy as jnp
import numpy as np
from jax import lax
from jax.experimental import pallas as pl
from jax.experimental.pallas import tpu as pltpu
from jax.sharding import PartitionSpec as P

STOPS = 8
MAPH = 256
LANES = 128
TILE = 16


def fit_turns():
    z = 0.125 - 0.125 * np.cos(np.pi * (np.arange(400) + 0.5) / 400)
    t = np.sqrt(z)
    cheb = np.polynomial.chebyshev.Chebyshev
    cos_fit = cheb.fit(z, np.cos(2 * np.pi * t), 7, domain=[0, 0.25])
    sin_fit = cheb.fit(z, np.sin(2 * np.pi * t) / t, 6, domain=[0, 0.25])
    power = np.polynomial.Polynomial
    return (
        [float(np.float32(c)) for c in cos_fit.convert(kind=power).coef],
        [float(np.float32(c)) for c in sin_fit.convert(kind=power).coef],
    )


COS_COEF, SIN_COEF = fit_turns()


def cos_sin_turns(turns):
    t = turns - jnp.round(turns)
    z = t * t
    c = jnp.full_like(z, COS_COEF[-1])
    for coef in COS_COEF[-2::-1]:
        c = c * z + coef
    s = jnp.full_like(z, SIN_COEF[-1])
    for coef in SIN_COEF[-2::-1]:
        s = s * z + coef
    return c, s * t


def iota(shape, axis):
    return lax.broadcasted_iota(jnp.int32, shape, axis)


def kernel(
    sizes,
    block_ref, curv_ref, weight_ref, tiles_ref, offs_ref, owner_ref,
    out_ref,
    blocks, ranges, cross, phased, right, x_send, x_recv, x_own, packed, arrived, slot_hot,
    o_send, o_recv, u_acc, v_acc,
    g_send, g_recv, xs_sem, xr_sem, as_sem, ar_sem, os_sem, or_sem,
):
    blk, maps, pulses, freqs, columns, rows, cap = sizes
    f32, bf16 = jnp.float32, jnp.bfloat16
    me = lax.axis_index("blk")
    my_map = lax.axis_index("map")
    other_map = 1 - my_map
    core = lax.rem(me, 2)
    span = STOPS * maps * pulses
    stacked = STOPS * pulses
    chunks = columns // LANES
    width = 2 * LANES
    slots = blk * cap
    own_stop = STOPS // 2 - 1

    def device(index):
        return (lax.rem(index + 2 * blk, blk), my_map)

    mesh_id = pl.DeviceIdType.MESH

    barrier = pltpu.get_barrier_semaphore()

    def greet(i, _):
        pl.semaphore_signal(barrier, inc=1, device_id=device(me + i), device_id_type=mesh_id)
        return 0

    lax.fori_loop(1, blk, greet, 0)
    pl.semaphore_signal(barrier, inc=1, device_id=(me, other_map), device_id_type=mesh_id)
    blocks[own_stop] = block_ref[...]
    pl.semaphore_wait(barrier, blk)

    def push(source, stop, target, sem):
        return pltpu.make_async_remote_copy(
            src_ref=source, dst_ref=blocks.at[stop], send_sem=g_send.at[sem],
            recv_sem=g_recv.at[stop], device_id=target, device_id_type=mesh_id)

    def arrived_block(stop):
        pltpu.make_async_copy(blocks.at[stop], blocks.at[stop], g_recv.at[stop]).wait()

    partner = device(me + 1 - 2 * core)
    shift = 2 * core - 1

    push(block_ref, 7, device(me - 4), 0).start()

    @pl.when(core == 1)
    def _():
        push(block_ref, 0, device(me + 3), 6).start()

    push(block_ref, 5, device(me - 2), 1).start()
    push(block_ref, 1, device(me + 2), 2).start()
    push(block_ref, own_stop + shift, partner, 3).start()

    def fill_ranges(i, _):
        at = pl.ds(pl.multiple_of(i * TILE, TILE), TILE)
        below = pl.ds(pl.multiple_of(freqs + i * TILE, TILE), TILE)
        f = (i * TILE + iota((TILE, columns), 0)).astype(f32)
        c = iota((TILE, columns), 1).astype(f32)
        re, im = cos_sin_turns(f * c * (1.0 / freqs))
        re = (re * (1.0 / math.sqrt(freqs))).astype(bf16)
        im = (im * (1.0 / math.sqrt(freqs)))
        pos, neg = im.astype(bf16), (-im).astype(bf16)
        for n in range(chunks):
            cut = slice(n * LANES, (n + 1) * LANES)
            ranges[n, at, 0:LANES] = re[:, cut]
            ranges[n, at, LANES:width] = neg[:, cut]
            ranges[n, below, 0:LANES] = pos[:, cut]
            ranges[n, below, LANES:width] = re[:, cut]
        return 0

    lax.fori_loop(0, freqs // TILE, fill_ranges, 0)

    curvature = curv_ref[0]

    def spectrum(k):
        first = (k * maps + my_map) * pulses

        def turn(i, _):
            at = pl.ds(pl.multiple_of(i * TILE, TILE), TILE)
            q = first + i * TILE + iota((TILE, freqs), 0)
            s = q.astype(f32) * (1.0 / span) - 0.5
            r = iota((TILE, freqs), 1).astype(f32) * (1.0 / freqs) - 0.5
            angle = curvature * (s * s) * (1.0 + r)
            c, si = cos_sin_turns(angle * (0.5 / math.pi))
            re = blocks[k, at, 0:freqs].astype(f32)
            im = blocks[k, at, freqs:2 * freqs].astype(f32)
            phased[at, 0:freqs] = (re * c - im * si).astype(bf16)
            phased[at, freqs:2 * freqs] = (re * si + im * c).astype(bf16)
            return 0

        lax.fori_loop(0, pulses // TILE, turn, 0)
        top = pl.ds(pl.multiple_of(k * pulses, pulses), pulses)
        low = pl.ds(pl.multiple_of(stacked + k * pulses, pulses), pulses)

        def chunk(n, _):
            y = jnp.dot(phased[...], ranges[n], preferred_element_type=f32)
            yr, yi = y[:, :LANES], y[:, LANES:]
            right[n, top, 0:LANES] = yr.astype(bf16)
            right[n, top, LANES:width] = yi.astype(bf16)
            right[n, low, 0:LANES] = (-yi).astype(bf16)
            right[n, low, LANES:width] = yr.astype(bf16)
            return 0

        lax.fori_loop(0, chunks, chunk, 0)

    def fill_cross():
        lane = iota((1, stacked), 1)
        q = (lane + (lax.div(lane, pulses) * (maps - 1) + my_map) * pulses).astype(f32)

        def fill(i, _):
            at = pl.ds(pl.multiple_of(i * TILE, TILE), TILE)
            a = (i * TILE + iota((TILE, stacked), 0)).astype(f32)
            re, im = cos_sin_turns(a * q * (1.0 / span))
            cross[at, 0:stacked] = (re * (1.0 / math.sqrt(span))).astype(bf16)
            cross[at, stacked:2 * stacked] = (im * (-1.0 / math.sqrt(span))).astype(bf16)
            return 0

        lax.fori_loop(0, rows * maps // TILE, fill, 0)

    def fill_slots():
        tiles = tiles_ref[...]
        holders = iota((blk, rows), 0)
        dest = jnp.sum(jnp.where(holders == tiles, owner_ref[...], 0), axis=0, keepdims=True)
        hot = (holders == dest).astype(f32)
        upto = (iota((rows, rows), 0) <= iota((rows, rows), 1)).astype(f32).astype(bf16)
        counts = jnp.dot(hot.astype(bf16), upto, preferred_element_type=f32)
        rank = jnp.sum(counts * hot, axis=0, keepdims=True).astype(jnp.int32) - 1
        slot = dest * cap + rank
        for i in range(slots // LANES):
            at = i * LANES + iota((LANES, rows), 0)
            slot_hot[i * LANES:(i + 1) * LANES, :] = (at == slot).astype(f32).astype(bf16)
        place = lax.rem(me, LANES // cap) * cap + rank
        marks = jnp.where(iota((LANES, rows), 0) == place, (offs_ref[...] + 1).astype(f32), 0.0)
        table = lax.dot_general(
            hot.astype(bf16), marks.astype(bf16), (((1,), (1,)), ((), ())),
            preferred_element_type=f32)
        for d in range(blk):
            o_send[d] = table[d:d + 1, :]
        o_recv[me] = o_send[me]

        def send(i, _):
            to = lax.rem(me + i, blk)
            pltpu.make_async_remote_copy(
                src_ref=o_send.at[to], dst_ref=o_recv.at[me], send_sem=os_sem,
                recv_sem=or_sem, device_id=(to, my_map), device_id_type=mesh_id).start()
            return 0

        lax.fori_loop(1, blk, send, 0)

    def step(i, _):
        k = jnp.where(i == 0, own_stop, 0)
        for at, stop in ((1, 4 - 2 * core), (2, 5), (3, 1), (4, 2 + 2 * core), (5, 7), (7, 6)):
            k = jnp.where(i == at, stop, k)

        @pl.when(i == 2)
        def _():
            arrived_block(5)
            push(blocks.at[5], 5 + shift, partner, 4).start()
            arrived_block(1)
            push(blocks.at[1], 1 + shift, partner, 5).start()

        @pl.when(i == 4)
        def _():
            arrived_block(7)

            @pl.when(core == 0)
            def _():
                push(blocks.at[7], 6, partner, 6).start()

        @pl.when((i == 1) | (i == 4) | (i == 6) | (i == 7))
        def _():
            arrived_block(k)

        spectrum(k)

        @pl.when(i == 0)
        def _():
            fill_slots()

        @pl.when(i == 1)
        def _():
            fill_cross()

        return 0

    lax.fori_loop(0, STOPS, step, 0)

    def x_copy(n):
        return pltpu.make_async_remote_copy(
            src_ref=x_send.at[n], dst_ref=x_recv.at[n], send_sem=xs_sem.at[n],
            recv_sem=xr_sem.at[n], device_id=(me, other_map), device_id_type=mesh_id)

    own_slots = pl.ds(pl.multiple_of(me * cap, cap), cap)

    def column_step(n, _):
        @pl.when(n < chunks)
        def _():
            theirs = cross[pl.ds(pl.multiple_of(other_map * rows, rows), rows), :]
            x_send[n] = jnp.dot(theirs, right[n], preferred_element_type=f32).astype(bf16)
            x_copy(n).start()
            mine = cross[pl.ds(pl.multiple_of(my_map * rows, rows), rows), :]
            x_own[n] = jnp.dot(mine, right[n], preferred_element_type=f32)

        @pl.when(n >= 1)
        def _():
            b = n - 1
            x_copy(b).wait_recv()
            image = (x_own[b] + x_recv[b].astype(f32)).astype(bf16)
            packed[b] = jnp.dot(slot_hot[...], image, preferred_element_type=f32).astype(bf16)

            def send(i, _):
                to = lax.rem(me + i, blk)
                pltpu.make_async_remote_copy(
                    src_ref=packed.at[b, pl.ds(pl.multiple_of(to * cap, cap), cap)],
                    dst_ref=arrived.at[b, own_slots], send_sem=as_sem.at[b],
                    recv_sem=ar_sem.at[b], device_id=(to, my_map),
                    device_id_type=mesh_id).start()
                return 0

            lax.fori_loop(1, blk, send, 0)
            arrived[b, own_slots, :] = packed[b, own_slots, :]

        return 0

    lax.fori_loop(0, chunks + 1, column_step, 0)

    def wait_bytes(ref, sem):
        pltpu.make_async_copy(ref, ref, sem).wait()

    others = pl.ds(0, (blk - 1) * cap)
    u_acc[...] = jnp.zeros_like(u_acc)
    v_acc[...] = jnp.zeros_like(v_acc)

    def interp(n, _):
        wait_bytes(arrived.at[n, others], ar_sem.at[n])
        w = weight_ref[pl.ds(pl.multiple_of(n * LANES, LANES), LANES), :]
        u_acc[...] += jnp.dot(arrived[n, :, 0:LANES], w, preferred_element_type=f32)
        v_acc[...] += jnp.dot(arrived[n, :, LANES:width], w, preferred_element_type=f32)
        return 0

    lax.fori_loop(0, chunks, interp, 0)
    wait_bytes(o_recv.at[pl.ds(0, blk - 1)], or_sem)
    per = LANES // cap
    pieces = []
    for g in range(blk // per):
        total = o_recv[g * per]
        for j in range(1, per):
            total = total + o_recv[g * per + j]
        pieces.append(total)
    total = jnp.zeros((MAPH, columns), f32)
    for g in range(slots // LANES):
        cut = slice(g * LANES, (g + 1) * LANES)
        spot = iota((MAPH, LANES), 0) == pieces[g].astype(jnp.int32) - 1
        spot = spot.astype(f32).astype(bf16)
        u, v = u_acc[cut, :], v_acc[cut, :]
        power = u * u + v * v
        high = power.astype(bf16)
        rest = power - high.astype(f32)
        mid = rest.astype(bf16)
        low = (rest - mid.astype(f32)).astype(bf16)
        for part in (high, mid, low):
            total = total + jnp.dot(spot, part, preferred_element_type=f32)
    out_ref[...] = total

    for sem in range(7):
        wait_bytes(blocks.at[0], g_send.at[sem])
    for n in range(chunks):
        wait_bytes(x_send.at[n], xs_sem.at[n])
        wait_bytes(packed.at[n, others], as_sem.at[n])
    wait_bytes(o_send.at[pl.ds(0, blk - 1)], os_sem)


def body(phase_history, tile_curvature, interp_weights, strip_tiles, row_offsets, tile_owner):
    blk = lax.axis_size("blk")
    maps = lax.axis_size("map")
    pulses = phase_history.shape[2]
    freqs = phase_history.shape[3] // 2
    columns = interp_weights.shape[2]
    rows = strip_tiles.shape[2]
    cap = max(TILE, 2 * rows // blk)
    slots = blk * cap
    chunks = columns // LANES
    width = 2 * LANES
    stacked = STOPS * pulses
    f32, bf16 = jnp.float32, jnp.bfloat16
    vmem = pl.BlockSpec(memory_space=pltpu.VMEM)
    dma = pltpu.SemaphoreType.DMA
    out = pl.pallas_call(
        functools.partial(kernel, (blk, maps, pulses, freqs, columns, rows, cap)),
        out_shape=jax.ShapeDtypeStruct((MAPH, columns), f32),
        in_specs=[vmem, pl.BlockSpec(memory_space=pltpu.SMEM), vmem, vmem, vmem, vmem],
        out_specs=vmem,
        scratch_shapes=[
            pltpu.VMEM((STOPS, pulses, 2 * freqs), bf16),
            pltpu.VMEM((chunks, 2 * freqs, width), bf16),
            pltpu.VMEM((rows * maps, 2 * stacked), bf16),
            pltpu.VMEM((pulses, 2 * freqs), bf16),
            pltpu.VMEM((chunks, 2 * stacked, width), bf16),
            pltpu.VMEM((chunks, rows, width), bf16),
            pltpu.VMEM((chunks, rows, width), bf16),
            pltpu.VMEM((chunks, rows, width), f32),
            pltpu.VMEM((chunks, slots, width), bf16),
            pltpu.VMEM((chunks, slots, width), bf16),
            pltpu.VMEM((slots, rows), bf16),
            pltpu.VMEM((blk, 1, LANES), f32),
            pltpu.VMEM((blk, 1, LANES), f32),
            pltpu.VMEM((slots, columns), f32),
            pltpu.VMEM((slots, columns), f32),
            dma((7,)), dma((STOPS,)), dma((chunks,)), dma((chunks,)),
            dma((chunks,)), dma((chunks,)), dma, dma,
        ],
        compiler_params=pltpu.CompilerParams(
            collective_id=0, has_side_effects=True, vmem_limit_bytes=60 * 2**20),
    )(
        phase_history[0, 0], tile_curvature, interp_weights[0],
        strip_tiles[0, 0].reshape(1, rows), row_offsets[0],
        tile_owner.reshape(blk, 1),
    )
    return out.reshape(1, 1, MAPH, columns)


def solution(mesh):
    in_specs = (
        P("blk", "map", None, None),
        P("blk"),
        P("blk", None, None),
        P("blk", "map", None, None),
        P("blk", "map", None),
        P(),
    )
    out_specs = P("blk", "map", None, None)
    return jax.shard_map(body, mesh=mesh, in_specs=in_specs, out_specs=out_specs, check_vma=False)
```

time: 144 us -> 65.5 us (0.45); the launches traced: 142 us -> 65.3 us
  Pallas kernels: 0 us -> 61.4 us
  waiting for transfers between devices: 56.7 us -> 0 us
  other arithmetic: 28.5 us -> 0 us
  starting transfers between devices: 26.4 us -> 0 us
  between operations: 14.6 us -> 0.67 us
  matrix products: 13.7 us -> 0 us
    pallas_call x0 -> x1, Pallas kernels: none -> 61.4 us  [body(): pl.pallas_call(functools.partial(kernel, (blk, maps, pulses, freqs, colum...]
    another operation x15 -> x0, other arithmetic: 27 us -> none
    reduce_scatter x1 -> x0, waiting for transfers between devices: 25.3 us -> none  [body(): lax.psum_scatter(running, 'map', scatter_dimension=0, tiled=True)]
    all_to_all x2 -> x0, waiting for transfers between devices: 21.6 us -> none  [the longest x1 21.6 us: body(): lax.all_to_all(packed, 'blk', split_axis=0, concat_axis=0, tiled=True)]
    ppermute x7 -> x0, starting transfers between devices: 14.8 us -> none  [from_behind(): return lax.ppermute(block, axis, route)]
    dot_general x19 -> x0, matrix products: 13.7 us -> none  [the longest x8 5.25 us: accumulate(): jnp.dot(left_side, right_side, preferred_element_type=jnp.float32)]
    all_to_all x2 -> x0, starting transfers between devices: 11.6 us -> none  [the longest x1 5.99 us: body(): lax.all_to_all(slot_offsets, 'blk', split_axis=0, concat_axis=0, tiled=True)]
    ppermute x7 -> x0, waiting for transfers between devices: 9.8 us -> none  [from_behind(): return lax.ppermute(block, axis, route)]
  transfers between devices with their start and end apart: 10 -> 0, of which waited for: 5 -> 0; matrix products, arithmetic and copies ran while one was open for 24% -> 0% of each run, Pallas kernels for 0% -> 0%
where the time goes in v1:
time: 65.5 us; the launch traced here: 65.3 us
  Pallas kernels  61.4 us (94%)
  local copies, waits for them, and re-layouts  3.2 us (5%)
  between operations  0.67 us (1%)
    pallas_call x1, Pallas kernels, body(): pl.pallas_call(functools.partial(kernel, (blk, maps, pulses, freqs, colum...  61.4 us
    unnamed x3, local copies, waits for them, and re-layouts  2.52 us

profile of v1, /device:TPU:0, one launch (start us, length us, event | category | flops | bytes accessed | tf_op | source)
XLA Modules:
  0.0 65.3 jit_solution(3422151122895182543)
XLA Ops:
  0.7 0.0 copy-start
  0.7 0.6 copy-done
  1.3 0.7 %copy.7.owner_ref = s32[16,1]{1,0:T(8,128)} copy(s32[16,1]{0,1:T(1,128)S(1)} %bitcast.11) | data formatting | bytes 128 | tf_op jit(solution)/shard_map/reshape | solution.py:371
  2.0 61.4 %shard_map.64 = f32[256,512]{1,0:T(8,128)} custom-call(bf16[128,1024]{1,0:T(8,128)(2,1)} %bitcast.8, f32[1]{0:T(128)S(6)} %copy.9.curv_ref, bf16[512,512]{1,0:T(8,128)(2,1)} %bitcast.7, s32[1,256]{1,0:T(1,128)} %bitcast.9, s32[1,256]{1,0:T(1,128)} %bitcast.10, s32[16,1]{1,0:T(8,128)} %copy.7.owner_ref), custom_call_target="tpu_custom_call" | custom-call | tf_op jit(solution)/shard_map/pallas_call | solution.py:342
  63.4 1.9 %copy.10 = f32[1,1,256,512]{3,2,1,0:T(8,128)} copy(f32[1,1,256,512]{3,2,1,0:T(8,128)} %bitcast.6) | data formatting | bytes 1048576
Async XLA Ops:
  0.7 0.7 %copy-start = (s32[16]{0:T(128)S(1)}, s32[16]{0:T(128)}, u32[]{:S(2)}) copy-start(s32[16]{0:T(128)} %param.11) | copy-start | bytes 196

commit v2 on v1

--- a/solution.py
+++ b/solution.py
@@ -51,7 +51,7 @@
     sizes,
     block_ref, curv_ref, weight_ref, tiles_ref, offs_ref, owner_ref,
     out_ref,
-    blocks, ranges, cross, phased, right, x_send, x_recv, x_own, packed, arrived, slot_hot,
+    blocks, ranges, cross, phased, right, weights, x_send, x_recv, x_own, packed, arrived, slot_hot,
     o_send, o_recv, u_acc, v_acc,
     g_send, g_recv, xs_sem, xr_sem, as_sem, ar_sem, os_sem, or_sem,
 ):
@@ -62,7 +62,7 @@
     other_map = 1 - my_map
     core = lax.rem(me, 2)
     span = STOPS * maps * pulses
-    stacked = STOPS * pulses
+    stacked = STOPS // 2 * pulses
     chunks = columns // LANES
     width = 2 * LANES
     slots = blk * cap
@@ -105,71 +105,49 @@
     push(block_ref, 1, device(me + 2), 2).start()
     push(block_ref, own_stop + shift, partner, 3).start()
 
+    half_freqs = freqs // 2
+    half_chunks = chunks // 2
+    half_rows = rows // 2
+
     def fill_ranges(i, _):
         at = pl.ds(pl.multiple_of(i * TILE, TILE), TILE)
-        below = pl.ds(pl.multiple_of(freqs + i * TILE, TILE), TILE)
-        f = (i * TILE + iota((TILE, columns), 0)).astype(f32)
-        c = iota((TILE, columns), 1).astype(f32)
-        re, im = cos_sin_turns(f * c * (1.0 / freqs))
-        re = (re * (1.0 / math.sqrt(freqs))).astype(bf16)
-        im = (im * (1.0 / math.sqrt(freqs)))
-        pos, neg = im.astype(bf16), (-im).astype(bf16)
-        for n in range(chunks):
-            cut = slice(n * LANES, (n + 1) * LANES)
-            ranges[n, at, 0:LANES] = re[:, cut]
-            ranges[n, at, LANES:width] = neg[:, cut]
-            ranges[n, below, 0:LANES] = pos[:, cut]
-            ranges[n, below, LANES:width] = re[:, cut]
-        return 0
-
-    lax.fori_loop(0, freqs // TILE, fill_ranges, 0)
-
-    curvature = curv_ref[0]
-
-    def spectrum(k):
-        first = (k * maps + my_map) * pulses
-
-        def turn(i, _):
-            at = pl.ds(pl.multiple_of(i * TILE, TILE), TILE)
-            q = first + i * TILE + iota((TILE, freqs), 0)
-            s = q.astype(f32) * (1.0 / span) - 0.5
-            r = iota((TILE, freqs), 1).astype(f32) * (1.0 / freqs) - 0.5
-            angle = curvature * (s * s) * (1.0 + r)
-            c, si = cos_sin_turns(angle * (0.5 / math.pi))
-            re = blocks[k, at, 0:freqs].astype(f32)
-            im = blocks[k, at, freqs:2 * freqs].astype(f32)
-            phased[at, 0:freqs] = (re * c - im * si).astype(bf16)
-            phased[at, freqs:2 * freqs] = (re * si + im * c).astype(bf16)
-            return 0
-
-        lax.fori_loop(0, pulses // TILE, turn, 0)
-        top = pl.ds(pl.multiple_of(k * pulses, pulses), pulses)
-        low = pl.ds(pl.multiple_of(stacked + k * pulses, pulses), pulses)
-
-        def chunk(n, _):
-            y = jnp.dot(phased[...], ranges[n], preferred_element_type=f32)
-            yr, yi = y[:, :LANES], y[:, LANES:]
-            right[n, top, 0:LANES] = yr.astype(bf16)
-            right[n, top, LANES:width] = yi.astype(bf16)
-            right[n, low, 0:LANES] = (-yi).astype(bf16)
-            right[n, low, LANES:width] = yr.astype(bf16)
-            return 0
-
-        lax.fori_loop(0, chunks, chunk, 0)
-
-    def fill_cross():
-        lane = iota((1, stacked), 1)
-        q = (lane + (lax.div(lane, pulses) * (maps - 1) + my_map) * pulses).astype(f32)
-
-        def fill(i, _):
-            at = pl.ds(pl.multiple_of(i * TILE, TILE), TILE)
-            a = (i * TILE + iota((TILE, stacked), 0)).astype(f32)
-            re, im = cos_sin_turns(a * q * (1.0 / span))
-            cross[at, 0:stacked] = (re * (1.0 / math.sqrt(span))).astype(bf16)
-            cross[at, stacked:2 * stacked] = (im * (-1.0 / math.sqrt(span))).astype(bf16)
-            return 0
-
-        lax.fori_loop(0, rows * maps // TILE, fill, 0)
+        below = pl.ds(pl.multiple_of(half_freqs + i * TILE, TILE), TILE)
+        f = (i * TILE + iota((TILE, columns // 2), 0)).astype(f32)
+        for odd in range(2):
+            c = (2 * iota((TILE, columns // 2), 1) + odd).astype(f32)
+            re, im = cos_sin_turns(f * c * (1.0 / freqs))
+            re = (re * (1.0 / math.sqrt(freqs))).astype(bf16)
+            im = (im * (1.0 / math.sqrt(freqs)))
+            pos, neg = im.astype(bf16), (-im).astype(bf16)
+            for n in range(half_chunks):
+                cut = slice(n * LANES, (n + 1) * LANES)
+                left = slice(n * width, n * width + LANES)
+                rest = slice(n * width + LANES, (n + 1) * width)
+                ranges[odd, at, left] = re[:, cut]
+                ranges[odd, at, rest] = neg[:, cut]
+                ranges[odd, below, left] = pos[:, cut]
+                ranges[odd, below, rest] = re[:, cut]
+        return 0
+
+    lax.fori_loop(0, half_freqs // TILE, fill_ranges, 0)
+
+    lane = iota((1, stacked), 1)
+    q_lane = (lane + (lax.div(lane, pulses) * (maps - 1) + my_map) * pulses).astype(f32)
+
+    def fill_cross(i, _):
+        at = pl.ds(pl.multiple_of(i * TILE, TILE), TILE)
+        g = i * TILE
+        odd = lax.div(g, rows)
+        own = lax.div(lax.rem(g, rows), half_rows)
+        part = jnp.where(own == 1, my_map, other_map)
+        base = part * rows + odd + 2 * lax.rem(g, half_rows)
+        a = (base + 2 * iota((TILE, stacked), 0)).astype(f32)
+        re, im = cos_sin_turns(a * q_lane * (1.0 / span))
+        cross[at, 0:stacked] = (re * (1.0 / math.sqrt(span))).astype(bf16)
+        cross[at, stacked:2 * stacked] = (im * (-1.0 / math.sqrt(span))).astype(bf16)
+        return 0
+
+    lax.fori_loop(0, rows * maps // TILE, fill_cross, 0)
 
     def fill_slots():
         tiles = tiles_ref[...]
@@ -180,9 +158,14 @@
         counts = jnp.dot(hot.astype(bf16), upto, preferred_element_type=f32)
         rank = jnp.sum(counts * hot, axis=0, keepdims=True).astype(jnp.int32) - 1
         slot = dest * cap + rank
+        spot = iota((rows, rows), 1)
+        spot = 2 * lax.rem(spot, half_rows) + lax.div(spot, half_rows)
+        order = (iota((rows, rows), 0) == spot).astype(f32).astype(bf16)
         for i in range(slots // LANES):
             at = i * LANES + iota((LANES, rows), 0)
-            slot_hot[i * LANES:(i + 1) * LANES, :] = (at == slot).astype(f32).astype(bf16)
+            hits = (at == slot).astype(f32).astype(bf16)
+            slot_hot[i * LANES:(i + 1) * LANES, :] = jnp.dot(
+                hits, order, preferred_element_type=f32).astype(bf16)
         place = lax.rem(me, LANES // cap) * cap + rank
         marks = jnp.where(iota((LANES, rows), 0) == place, (offs_ref[...] + 1).astype(f32), 0.0)
         table = lax.dot_general(
@@ -201,19 +184,78 @@
 
         lax.fori_loop(1, blk, send, 0)
 
+    fill_slots()
+
+    def order_weights(i, _):
+        at = pl.ds(pl.multiple_of(i * LANES, LANES), LANES)
+        r = i * LANES + iota((LANES, columns), 0)
+        r = 2 * lax.rem(r, columns // 2) + lax.div(r, columns // 2)
+        order = (iota((LANES, columns), 1) == r).astype(f32).astype(bf16)
+        weights[at, :] = jnp.dot(
+            order, weight_ref[...], preferred_element_type=f32).astype(bf16)
+        return 0
+
+    lax.fori_loop(0, chunks, order_weights, 0)
+
+    curvature = curv_ref[0]
+
+    def turned(k, i):
+        at = pl.ds(pl.multiple_of(i * TILE, TILE), TILE)
+        q = (k * maps + my_map) * pulses + i * TILE + iota((TILE, freqs), 0)
+        s = q.astype(f32) * (1.0 / span) - 0.5
+        r = iota((TILE, freqs), 1).astype(f32) * (1.0 / freqs) - 0.5
+        angle = curvature * (s * s) * (1.0 + r)
+        c, si = cos_sin_turns(angle * (0.5 / math.pi))
+        re = blocks[k, at, 0:freqs].astype(f32)
+        im = blocks[k, at, freqs:2 * freqs].astype(f32)
+        return re * c - im * si, re * si + im * c
+
+    def spectrum(j):
+        def turn(i, _):
+            first = turned(j, i)
+            second = turned(j + STOPS // 2, i)
+            for part in range(2):
+                z_sum, z_diff = first[part] + second[part], first[part] - second[part]
+                to = slice(part * half_freqs, (part + 1) * half_freqs)
+                for odd_row, z in ((0, z_sum), (1, z_diff)):
+                    at = pl.ds(pl.multiple_of(odd_row * pulses + i * TILE, TILE), TILE)
+                    near, far = z[:, :half_freqs], z[:, half_freqs:]
+                    phased[0, at, to] = (near + far).astype(bf16)
+                    phased[1, at, to] = (near - far).astype(bf16)
+            return 0
+
+        lax.fori_loop(0, pulses // TILE, turn, 0)
+        top = pl.ds(pl.multiple_of(j * pulses, pulses), pulses)
+        low = pl.ds(pl.multiple_of(stacked + j * pulses, pulses), pulses)
+
+        def columns_of(odd, _):
+            y = jnp.dot(phased[odd], ranges[odd], preferred_element_type=f32)
+            for h in range(half_chunks):
+                n = odd * half_chunks + h
+                yr = y[:, h * width:h * width + LANES]
+                yi = y[:, h * width + LANES:(h + 1) * width]
+                for odd_row in range(2):
+                    cut = slice(odd_row * pulses, (odd_row + 1) * pulses)
+                    real, imag = yr[cut].astype(bf16), yi[cut].astype(bf16)
+                    right[n, odd_row, top, 0:LANES] = real
+                    right[n, odd_row, top, LANES:width] = imag
+                    right[n, odd_row, low, 0:LANES] = (-yi[cut]).astype(bf16)
+                    right[n, odd_row, low, LANES:width] = real
+            return 0
+
+        lax.fori_loop(0, 2, columns_of, 0)
+
     def step(i, _):
-        k = jnp.where(i == 0, own_stop, 0)
-        for at, stop in ((1, 4 - 2 * core), (2, 5), (3, 1), (4, 2 + 2 * core), (5, 7), (7, 6)):
-            k = jnp.where(i == at, stop, k)
-
-        @pl.when(i == 2)
+        j = jnp.where(i == 0, 1, jnp.where(i == 1, 3, jnp.where(i == 2, 0, 2)))
+
+        @pl.when(i == 0)
         def _():
             arrived_block(5)
             push(blocks.at[5], 5 + shift, partner, 4).start()
             arrived_block(1)
             push(blocks.at[1], 1 + shift, partner, 5).start()
 
-        @pl.when(i == 4)
+        @pl.when(i == 1)
         def _():
             arrived_block(7)
 
@@ -221,23 +263,15 @@
             def _():
                 push(blocks.at[7], 6, partner, 6).start()
 
-        @pl.when((i == 1) | (i == 4) | (i == 6) | (i == 7))
+        @pl.when(i >= 2)
         def _():
-            arrived_block(k)
-
-        spectrum(k)
-
-        @pl.when(i == 0)
-        def _():
-            fill_slots()
-
-        @pl.when(i == 1)
-        def _():
-            fill_cross()
-
-        return 0
-
-    lax.fori_loop(0, STOPS, step, 0)
+            arrived_block(j)
+            arrived_block(j + STOPS // 2)
+
+        spectrum(j)
+        return 0
+
+    lax.fori_loop(0, STOPS // 2, step, 0)
 
     def x_copy(n):
         return pltpu.make_async_remote_copy(
@@ -249,11 +283,13 @@
     def column_step(n, _):
         @pl.when(n < chunks)
         def _():
-            theirs = cross[pl.ds(pl.multiple_of(other_map * rows, rows), rows), :]
-            x_send[n] = jnp.dot(theirs, right[n], preferred_element_type=f32).astype(bf16)
+            for odd_row in range(2):
+                table = cross[odd_row * rows:(odd_row + 1) * rows, :]
+                y = jnp.dot(table, right[n, odd_row], preferred_element_type=f32)
+                to = slice(odd_row * half_rows, (odd_row + 1) * half_rows)
+                x_send[n, to, :] = y[:half_rows].astype(bf16)
+                x_own[n, to, :] = y[half_rows:]
             x_copy(n).start()
-            mine = cross[pl.ds(pl.multiple_of(my_map * rows, rows), rows), :]
-            x_own[n] = jnp.dot(mine, right[n], preferred_element_type=f32)
 
         @pl.when(n >= 1)
         def _():
@@ -287,7 +323,7 @@
 
     def interp(n, _):
         wait_bytes(arrived.at[n, others], ar_sem.at[n])
-        w = weight_ref[pl.ds(pl.multiple_of(n * LANES, LANES), LANES), :]
+        w = weights[pl.ds(pl.multiple_of(n * LANES, LANES), LANES), :]
         u_acc[...] += jnp.dot(arrived[n, :, 0:LANES], w, preferred_element_type=f32)
         v_acc[...] += jnp.dot(arrived[n, :, LANES:width], w, preferred_element_type=f32)
         return 0
@@ -335,7 +371,7 @@
     slots = blk * cap
     chunks = columns // LANES
     width = 2 * LANES
-    stacked = STOPS * pulses
+    stacked = STOPS // 2 * pulses
     f32, bf16 = jnp.float32, jnp.bfloat16
     vmem = pl.BlockSpec(memory_space=pltpu.VMEM)
     dma = pltpu.SemaphoreType.DMA
@@ -346,10 +382,11 @@
         out_specs=vmem,
         scratch_shapes=[
             pltpu.VMEM((STOPS, pulses, 2 * freqs), bf16),
-            pltpu.VMEM((chunks, 2 * freqs, width), bf16),
+            pltpu.VMEM((2, freqs, columns), bf16),
             pltpu.VMEM((rows * maps, 2 * stacked), bf16),
-            pltpu.VMEM((pulses, 2 * freqs), bf16),
-            pltpu.VMEM((chunks, 2 * stacked, width), bf16),
+            pltpu.VMEM((2, 2 * pulses, freqs), bf16),
+            pltpu.VMEM((chunks, 2, 2 * stacked, width), bf16),
+            pltpu.VMEM((columns, columns), bf16),
             pltpu.VMEM((chunks, rows, width), bf16),
             pltpu.VMEM((chunks, rows, width), bf16),
             pltpu.VMEM((chunks, rows, width), f32),

time: 65.5 us -> 63.2 us (0.965)
  Pallas kernels: 61.4 us -> 59.2 us
    pallas_call x1, Pallas kernels: 61.4 us -> 59.2 us  [body(): pl.pallas_call(functools.partial(kernel, (blk, maps, pulses, freqs, colum...]
where the time goes in v2:
time: 63.2 us; the launch traced here: 63 us
  Pallas kernels  59.2 us (94%)
  local copies, waits for them, and re-layouts  3.2 us (5%)
  between operations  0.67 us (1%)
    pallas_call x1, Pallas kernels, body(): pl.pallas_call(functools.partial(kernel, (blk, maps, pulses, freqs, colum...  59.2 us
    unnamed x3, local copies, waits for them, and re-layouts  2.52 us

profile of v2, /device:TPU:0, one launch (start us, length us, event | category | flops | bytes accessed | tf_op | source)
XLA Modules:
  0.0 63.0 jit_solution(7378111808433693706)
XLA Ops:
  0.7 0.0 copy-start
  0.7 0.6 %copy-done = s32[16]{0:T(128)S(1)} copy-done((s32[16]{0:T(128)S(1)}, s32[16]{0:T(128)}, u32[]{:S(2)}) %copy-start) | copy-done | bytes 88
  1.3 0.7 %copy.7.owner_ref = s32[16,1]{1,0:T(8,128)} copy(s32[16,1]{0,1:T(1,128)S(1)} %bitcast.11) | data formatting | bytes 128 | tf_op jit(solution)/shard_map/reshape | solution.py:408
  2.0 59.2 %shard_map.64 = f32[256,512]{1,0:T(8,128)} custom-call(bf16[128,1024]{1,0:T(8,128)(2,1)} %bitcast.8, f32[1]{0:T(128)S(6)} %copy.9.curv_ref, bf16[512,512]{1,0:T(8,128)(2,1)} %bitcast.7, s32[1,256]{1,0:T(1,128)} %bitcast.9, s32[1,256]{1,0:T(1,128)} %bitcast.10, s32[16,1]{1,0:T(8,128)} %copy.7.owner_ref), custom_call_target="tpu_custom_call" | custom-call | tf_op jit(solution)/shard_map/pallas_call | solution.py:378
  61.2 1.9 %copy.10 = f32[1,1,256,512]{3,2,1,0:T(8,128)} copy(f32[1,1,256,512]{3,2,1,0:T(8,128)} %bitcast.6) | data formatting | bytes 1048576
Async XLA Ops:
  0.7 0.7 %copy-start = (s32[16]{0:T(128)S(1)}, s32[16]{0:T(128)}, u32[]{:S(2)}) copy-start(s32[16]{0:T(128)} %param.11) | copy-start | bytes 196

commit v3 on v2

--- a/solution.py
+++ b/solution.py
@@ -121,12 +121,11 @@
             pos, neg = im.astype(bf16), (-im).astype(bf16)
             for n in range(half_chunks):
                 cut = slice(n * LANES, (n + 1) * LANES)
-                left = slice(n * width, n * width + LANES)
-                rest = slice(n * width + LANES, (n + 1) * width)
-                ranges[odd, at, left] = re[:, cut]
-                ranges[odd, at, rest] = neg[:, cut]
-                ranges[odd, below, left] = pos[:, cut]
-                ranges[odd, below, rest] = re[:, cut]
+                to = odd * half_chunks + n
+                ranges[to, at, 0:LANES] = re[:, cut]
+                ranges[to, at, LANES:width] = neg[:, cut]
+                ranges[to, below, 0:LANES] = pos[:, cut]
+                ranges[to, below, LANES:width] = re[:, cut]
         return 0
 
     lax.fori_loop(0, half_freqs // TILE, fill_ranges, 0)
@@ -152,8 +151,10 @@
     def fill_slots():
         tiles = tiles_ref[...]
         holders = iota((blk, rows), 0)
-        dest = jnp.sum(jnp.where(holders == tiles, owner_ref[...], 0), axis=0, keepdims=True)
-        hot = (holders == dest).astype(f32)
+        named = (holders == tiles).astype(f32).astype(bf16)
+        holds = (iota((blk, blk), 0) == owner_ref[...]).astype(f32).astype(bf16)
+        hot = jnp.dot(holds, named, preferred_element_type=f32)
+        dest = jnp.sum(holders.astype(f32) * hot, axis=0, keepdims=True).astype(jnp.int32)
         upto = (iota((rows, rows), 0) <= iota((rows, rows), 1)).astype(f32).astype(bf16)
         counts = jnp.dot(hot.astype(bf16), upto, preferred_element_type=f32)
         rank = jnp.sum(counts * hot, axis=0, keepdims=True).astype(jnp.int32) - 1
@@ -224,26 +225,24 @@
                     phased[1, at, to] = (near - far).astype(bf16)
             return 0
 
-        lax.fori_loop(0, pulses // TILE, turn, 0)
+        lax.fori_loop(0, pulses // TILE, turn, 0, unroll=2)
         top = pl.ds(pl.multiple_of(j * pulses, pulses), pulses)
         low = pl.ds(pl.multiple_of(stacked + j * pulses, pulses), pulses)
 
-        def columns_of(odd, _):
-            y = jnp.dot(phased[odd], ranges[odd], preferred_element_type=f32)
-            for h in range(half_chunks):
-                n = odd * half_chunks + h
-                yr = y[:, h * width:h * width + LANES]
-                yi = y[:, h * width + LANES:(h + 1) * width]
-                for odd_row in range(2):
-                    cut = slice(odd_row * pulses, (odd_row + 1) * pulses)
-                    real, imag = yr[cut].astype(bf16), yi[cut].astype(bf16)
-                    right[n, odd_row, top, 0:LANES] = real
-                    right[n, odd_row, top, LANES:width] = imag
-                    right[n, odd_row, low, 0:LANES] = (-yi[cut]).astype(bf16)
-                    right[n, odd_row, low, LANES:width] = real
+        def columns_of(n, _):
+            odd = lax.div(n, half_chunks)
+            y = jnp.dot(phased[odd], ranges[n], preferred_element_type=f32)
+            yr, yi = y[:, :LANES], y[:, LANES:]
+            for odd_row in range(2):
+                cut = slice(odd_row * pulses, (odd_row + 1) * pulses)
+                real, imag = yr[cut].astype(bf16), yi[cut].astype(bf16)
+                right[n, odd_row, top, 0:LANES] = real
+                right[n, odd_row, top, LANES:width] = imag
+                right[n, odd_row, low, 0:LANES] = (-yi[cut]).astype(bf16)
+                right[n, odd_row, low, LANES:width] = real
             return 0
 
-        lax.fori_loop(0, 2, columns_of, 0)
+        lax.fori_loop(0, chunks, columns_of, 0, unroll=True)
 
     def step(i, _):
         j = jnp.where(i == 0, 1, jnp.where(i == 1, 3, jnp.where(i == 2, 0, 2)))
@@ -328,7 +327,7 @@
         v_acc[...] += jnp.dot(arrived[n, :, LANES:width], w, preferred_element_type=f32)
         return 0
 
-    lax.fori_loop(0, chunks, interp, 0)
+    lax.fori_loop(0, chunks, interp, 0, unroll=True)
     wait_bytes(o_recv.at[pl.ds(0, blk - 1)], or_sem)
     per = LANES // cap
     pieces = []
@@ -382,7 +381,7 @@
         out_specs=vmem,
         scratch_shapes=[
             pltpu.VMEM((STOPS, pulses, 2 * freqs), bf16),
-            pltpu.VMEM((2, freqs, columns), bf16),
+            pltpu.VMEM((chunks, freqs, width), bf16),
             pltpu.VMEM((rows * maps, 2 * stacked), bf16),
             pltpu.VMEM((2, 2 * pulses, freqs), bf16),
             pltpu.VMEM((chunks, 2, 2 * stacked, width), bf16),
@@ -405,9 +404,9 @@
     )(
         phase_history[0, 0], tile_curvature, interp_weights[0],
         strip_tiles[0, 0].reshape(1, rows), row_offsets[0],
-        tile_owner.reshape(blk, 1),
+        tile_owner.reshape(1, blk),
     )
-    return out.reshape(1, 1, MAPH, columns)
+    return jnp.maximum(out, 0.0).reshape(1, 1, MAPH, columns)
 
 
 def solution(mesh):

time: 63.2 us -> 61 us (0.965)
  local copies, waits for them, and re-layouts: 3.2 us -> 0 us
  other arithmetic: 0 us -> 1.88 us
  Pallas kernels: 59.2 us -> 58.3 us
    unnamed x3 -> x0, local copies, waits for them, and re-layouts: 2.52 us -> none
    reshape x0 -> x1, other arithmetic: none -> 1.88 us  [body(): return jnp.maximum(out, 0.0).reshape(1, 1, MAPH, columns)]
    pallas_call x1, Pallas kernels: 59.2 us -> 58.3 us  [body(): pl.pallas_call(functools.partial(kernel, (blk, maps, pulses, freqs, colum...]
    reshape x1 -> x0, local copies, waits for them, and re-layouts: 0.68 us -> none  [body(): tile_owner.reshape(blk, 1)]
where the time goes in v3:
time: 61 us; the launch traced here: 60.8 us
  Pallas kernels  58.3 us (96%)
  other arithmetic  1.88 us (3%)
  between operations  0.66 us (1%)
    pallas_call x1, Pallas kernels, body(): pl.pallas_call(functools.partial(kernel, (blk, maps, pulses, freqs, colum...  58.3 us
    reshape x1, other arithmetic, body(): return jnp.maximum(out, 0.0).reshape(1, 1, MAPH, columns)  1.88 us

profile of v3, /device:TPU:0, one launch (start us, length us, event | category | flops | bytes accessed | tf_op | source)
XLA Modules:
  0.0 60.8 jit_solution(1692428803008701477)
XLA Ops:
  0.7 58.3 %shard_map.64 = f32[256,512]{1,0:T(8,128)} custom-call(bf16[128,1024]{1,0:T(8,128)(2,1)} %bitcast.8, f32[1]{0:T(128)S(6)} %copy.7.curv_ref, bf16[512,512]{1,0:T(8,128)(2,1)} %bitcast.7, s32[1,256]{1,0:T(1,128)} %bitcast.9, s32[1,256]{1,0:T(1,128)} %bitcast.10, s32[1,16]{1,0:T(1,128)} %bitcast.11), custom_call_target="tpu_custom_call" | custom-call | tf_op jit(solution)/shard_map/pallas_call | solution.py:377
  58.9 1.9 %maximum_bitcast_fusion = f32[1,1,256,512]{3,2,1,0:T(8,128)} fusion(f32[256,512]{1,0:T(8,128)} %shard_map.64), kind=kLoop, calls=%fused_computation | loop fusion | flops 131072 | bytes 1048576 | tf_op jit(solution)/shard_map/reshape | solution.py:409
